TPU v7x, 256 devices: a whole 4x4x8 slice. The times are simulated.
256 devices in a mesh: seq: 128 (over y_lo, x, z, core), req: 2 (over y_hi).
Axes of the slice: x: 4, y: 4 (y_hi: 2, y_lo: 2; y = y_hi * 2 + y_lo), z: 8, core: 2. Of those that a mesh axis runs over, the one named last changes fastest.
Arguments:
- tokens: bfloat16 [16384, 2048], P('seq'), may hold values from -6 to 6
- norm_gain: float32 [2048], replicated, may hold values from 0.5 to 1.5
- w_query: bfloat16 [2048, 1024], P(None, 'req'), as said below
- key_projection: bfloat16 [2048, 512], P(None, 'req')
- value_projection: bfloat16 [2048, 512], P(None, 'req'), may hold values from -0.125 to 0.125
- w_out: bfloat16 [1024, 2048], P('req'), may hold values from -0.1875 to 0.1875
- lengths: int32 [4], replicated, may hold values from 1 to 10922, 16384 in all
- block_split: int32 [128], replicated, may hold values from 0 to 127, each once
- page_slot: int32 [512], replicated, may hold values from 0 to 1023, as said below
Outputs:
- hidden: bfloat16 [16384, 2048], P(('seq', 'req'))
- key_value_cache: bfloat16 [1024, 2, 32, 512], P('seq', None, None, 'req')
Inputs may be any that keep to these rules, and one draw needn't show every extreme that they name: block_split is a permutation; index i of seq holds block block_split[i] and its mirror. `page_slot`: distinct slots; slot s lies on index s // 8 of seq. `w_query`: a projection scaled like 2 / sqrt(2048).
All inputs are finite; a program needn't handle non-finite values.
Results may differ from a plain program's by a relative error of at most 0.014.
The roundings to bfloat16 on the way count: a program that leaves them out, or rounds other values in their place, can miss the bound.
Values may be sent and summed in bfloat16 or wider, within the bound.
A program may use at most 128 MiB of HBM per device.

v0:
```python
import math
import jax
import jax.numpy as jnp
from jax import lax
from jax.sharding import PartitionSpec as P

HEAD_SIZE = 128
PAGE_TOKENS = 32
theta_base = 1000000.0
norm_eps = 1e-05
far_below = -1e30


def rotary_rows(heads, offset_list):
    half_width = heads.shape[-1] // 2
    exponent = jnp.arange(half_width, dtype=jnp.float32) * (2.0 / heads.shape[-1])
    inv_freq = jnp.power(theta_base, -exponent)
    angle = offset_list.astype(jnp.float32)[:, None] * inv_freq[None, :]
    cosine = jnp.concatenate([jnp.cos(angle), jnp.cos(angle)], -1)[:, None, :]
    sine = jnp.concatenate([jnp.sin(angle), jnp.sin(angle)], -1)[:, None, :]
    rolled = jnp.concatenate([-heads[..., half_width:], heads[..., :half_width]], -1)
    return heads * cosine + rolled * sine


def slot_positions(block_split, lengths, total_rows, shard_rows):
    row_ids = jnp.arange(total_rows, dtype=jnp.int32)
    half_rows = shard_rows // 2
    cycle_size = block_split.shape[0]
    owner_dev = row_ids // shard_rows
    device_ids = jnp.arange(cycle_size, dtype=jnp.int32)
    first_block = jnp.sum(
        jnp.where(owner_dev[:, None] == device_ids[None, :], block_split[None, :], 0), 1
    )
    block_ids = jnp.where(
        row_ids % shard_rows < half_rows, first_block, 2 * cycle_size - 1 - first_block
    )
    position = block_ids * half_rows + row_ids % half_rows
    request_ends = jnp.cumsum(lengths)
    request_begins = request_ends - lengths
    request = jnp.sum((position[:, None] >= request_ends[None, :]).astype(jnp.int32), 1)
    prompt_ids = jnp.arange(lengths.shape[0], dtype=jnp.int32)
    begins = jnp.sum(
        jnp.where(request[:, None] == prompt_ids[None, :], request_begins[None, :], 0), 1
    )
    return (position, request, position - begins)


def on_device(
    tokens,
    norm_gain,
    w_query,
    key_projection,
    value_projection,
    w_out,
    lengths,
    block_split,
    page_slot,
):
    shard_rows = tokens.shape[0]
    half_rows = shard_rows // 2
    cycle_size = lax.axis_size("seq")
    device = lax.axis_index("seq")
    first_row = device * shard_rows
    position, request, offset_list = slot_positions(
        block_split, lengths, shard_rows * cycle_size, shard_rows
    )
    q_pos = lax.dynamic_slice_in_dim(position, first_row, shard_rows, 0)
    q_req = lax.dynamic_slice_in_dim(request, first_row, shard_rows, 0)
    q_off = lax.dynamic_slice_in_dim(offset_list, first_row, shard_rows, 0)
    cache_rows = 2 * shard_rows
    slot_count = cache_rows // PAGE_TOKENS
    slot_ids = page_slot[position // PAGE_TOKENS]
    holder = slot_ids // slot_count
    target_rows = jnp.where(
        holder == device, slot_ids % slot_count * PAGE_TOKENS + position % PAGE_TOKENS, -1
    )
    heads_local = w_query.shape[1] // HEAD_SIZE
    kv_local = key_projection.shape[1] // HEAD_SIZE
    group_width = heads_local // kv_local
    scale_factor = 1.0 / math.sqrt(HEAD_SIZE)
    widened = tokens.astype(jnp.float32)
    normalized_input = (
        widened * lax.rsqrt(jnp.mean(widened * widened, -1, keepdims=True) + norm_eps) * norm_gain
    ).astype(jnp.bfloat16)
    queries = rotary_rows(
        jnp.dot(normalized_input, w_query, preferred_element_type=jnp.float32).reshape(
            shard_rows, heads_local, HEAD_SIZE
        ),
        q_off,
    )
    queries = queries.astype(jnp.bfloat16).reshape(shard_rows, kv_local, group_width, HEAD_SIZE)
    key_matrix_rows = rotary_rows(
        jnp.dot(normalized_input, key_projection, preferred_element_type=jnp.float32).reshape(
            shard_rows, kv_local, HEAD_SIZE
        ),
        q_off,
    )
    key_matrix_rows = key_matrix_rows.astype(jnp.bfloat16).reshape(shard_rows, kv_local * HEAD_SIZE)
    value_matrix_rows = jnp.dot(
        normalized_input, value_projection, preferred_element_type=jnp.float32
    ).astype(jnp.bfloat16)

    def attend(moments, key_block, value_block, visible):
        run_max, run_sum, run_acc = moments
        width = key_block.shape[0]
        key_heads = key_block.reshape(width, kv_local, HEAD_SIZE)
        value_heads = value_block.reshape(width, kv_local, HEAD_SIZE)
        scores = (
            jnp.einsum("qhgd,khd->hgqk", queries, key_heads, preferred_element_type=jnp.float32)
            * scale_factor
        )
        masked = jnp.where(visible[None, None], scores, far_below)
        new_max = jnp.maximum(run_max, jnp.max(masked, -1))
        weights = jnp.where(visible[None, None], jnp.exp(masked - new_max[..., None]), 0.0)
        factor = jnp.exp(run_max - new_max)
        new_sum = run_sum * factor + jnp.sum(weights, -1)
        added = jnp.einsum(
            "hgqk,khd->hgqd",
            weights.astype(jnp.bfloat16),
            value_heads,
            preferred_element_type=jnp.float32,
        )
        return (new_max, new_sum, run_acc * factor[..., None] + added)

    def store(parts, key_block, value_block, key_target):
        cache_grid = jnp.arange(cache_rows, dtype=jnp.int32)
        placer = (cache_grid[:, None] == key_target[None, :]).astype(jnp.bfloat16)
        return (
            parts[0] + jnp.dot(placer, key_block, preferred_element_type=jnp.float32),
            parts[1] + jnp.dot(placer, value_block, preferred_element_type=jnp.float32),
        )

    start_max = jnp.full((kv_local, group_width, shard_rows), far_below, jnp.float32)
    start_sum = jnp.zeros((kv_local, group_width, shard_rows), jnp.float32)
    start_acc = jnp.zeros((kv_local, group_width, shard_rows, HEAD_SIZE), jnp.float32)
    start_keys = jnp.zeros((cache_rows, kv_local * HEAD_SIZE), jnp.float32)
    start_values = jnp.zeros((cache_rows, kv_local * HEAD_SIZE), jnp.float32)
    state = (start_max, start_sum, start_acc, start_keys, start_values)
    absorb_state = state
    key_piece = lax.all_gather(key_matrix_rows, "seq", axis=0, tiled=True)
    value_piece = lax.all_gather(value_matrix_rows, "seq", axis=0, tiled=True)
    length = key_piece.shape[0]
    sub_width = math.gcd(length, 1024)

    def sub_step(carried, sub_index):
        offset = sub_index * sub_width
        key_block = lax.dynamic_slice_in_dim(key_piece, offset, sub_width, 0)
        value_block = lax.dynamic_slice_in_dim(value_piece, offset, sub_width, 0)
        key_pos = lax.dynamic_slice_in_dim(position, offset, sub_width, 0)
        key_req = lax.dynamic_slice_in_dim(request, offset, sub_width, 0)
        key_target = lax.dynamic_slice_in_dim(target_rows, offset, sub_width, 0)
        visible = (key_req[None, :] == q_req[:, None]) & (key_pos[None, :] <= q_pos[:, None])
        moments = carried[:3]
        cache_parts = carried[3:]
        moments = attend(moments, key_block, value_block, visible)
        cache_parts = lax.cond(
            jnp.any(key_target >= 0),
            store,
            lambda parts, key_block, value_block, key_target: parts,
            cache_parts,
            key_block,
            value_block,
            key_target,
        )
        return (moments + cache_parts, None)

    absorb_state, _ = lax.scan(
        sub_step, absorb_state, jnp.arange(length // sub_width, dtype=jnp.int32)
    )
    state = absorb_state
    run_max, run_sum, run_acc, cache_keys, cache_values = state
    normalised = run_acc / run_sum[..., None]
    context = (
        jnp.transpose(normalised, (2, 0, 1, 3))
        .reshape(shard_rows, heads_local * HEAD_SIZE)
        .astype(jnp.bfloat16)
    )
    summed = lax.psum_scatter(
        jnp.dot(context, w_out, preferred_element_type=jnp.float32).astype(jnp.bfloat16),
        "req",
        scatter_dimension=0,
        tiled=True,
    ).astype(jnp.float32)
    residual = lax.dynamic_slice_in_dim(tokens, lax.axis_index("req") * half_rows, half_rows, 0)
    hidden = (summed + residual.astype(jnp.float32)).astype(jnp.bfloat16)
    key_value_cache = jnp.stack(
        [
            cache_keys.reshape(slot_count, PAGE_TOKENS, kv_local * HEAD_SIZE),
            cache_values.reshape(slot_count, PAGE_TOKENS, kv_local * HEAD_SIZE),
        ],
        1,
    ).astype(jnp.bfloat16)
    return (hidden, key_value_cache)


def solution(mesh):
    in_specs = (
        P("seq", None),
        P(),
        P(None, "req"),
        P(None, "req"),
        P(None, "req"),
        P("req", None),
        P(),
        P(),
        P(),
    )
    out_specs = (P(("seq", "req"), None), P("seq", None, None, "req"))
    return jax.shard_map(
        on_device, mesh=mesh, in_specs=in_specs, out_specs=out_specs, check_vma=False
    )
```

profile of v0, /device:TPU:1, one launch (start us, length us, event | category | flops | bytes accessed | tf_op | source)
XLA Modules:
  0.0 716.6 jit_solution(10461966883109596945)
XLA Ops:
  8.7 2.4 convolution_convert_fusion.1
  13.0 5.1 select_reduce_fusion
  18.6 101.9 %gather_fusion = s32[16384]{0:T(1024)S(1)} fusion(s32[512]{0:T(512)S(1)} %copy-done.1, s32[16384]{0:T(1024)S(1)} %broadcast_clamp_fusion), kind=kCustom, calls=%fused_computation | custom fusion | bytes 196608 | tf_op jit(solution)/shard_map/gather | solution.py:72
  124.2 2.1 fusion.42
  127.7 107.3 %all-gather.5.cloned.1.call-done = bf16[16384,256]{1,0:T(8,128)(2,1)} async-done(((bf16[128,256]{1,0:T(8,128)(2,1)}), bf16[16384,256]{1,0:T(8,128)(2,1)}) %all-gather.5.cloned.1.call-update) | async-done | bytes 8388624 | tf_op jit(solution)/shard_map/all_gather | solution.py:141
  235.0 222.0 %all-gather.3.cloned.1.call-done = bf16[16384,256]{1,0:T(8,128)(2,1)} async-done(((bf16[128,256]{1,0:T(8,128)(2,1)}), bf16[16384,256]{1,0:T(8,128)(2,1)}) %all-gather.3.cloned.1.call-update) | async-done | bytes 8388624 | tf_op jit(solution)/shard_map/all_gather | solution.py:140
  458.4 229.8 %while.19 = (s32[]{:T(128)}, f32[2,2,128]{2,1,0:T(2,128)S(1)}, f32[2,2,128]{2,1,0:T(2,128)S(1)}, f32[2,2,128,128]{3,2,1,0:T(8,128)}, f32[256,256]{1,0:T(8,128)},...) while((s32[]{:T(128)}, f32[2,2,128]{2,1,0:T(2,128)S(1)}, ...), condition=%wide.region_11.12_spmd.clone, body=%wide.region_5.11_spmd.clone.sunk | while | flops 544936448 | bytes 20653632 | solution.py:167
  463.4 2.1 constant_dynamic-slice_fusion.3
  476.5 2.1 constant_dynamic-slice_fusion.3
  515.7 2.1 constant_dynamic-slice_fusion.3
  520.1 3.5 conditional.3
  535.7 3.5 conditional.3
  547.0 2.1 constant_dynamic-slice_fusion.3
  564.5 3.5 conditional.3
  575.8 2.1 constant_dynamic-slice_fusion.3
  580.1 3.5 conditional.3
  591.4 2.1 constant_dynamic-slice_fusion.3
  595.8 3.5 conditional.3
  607.1 2.1 constant_dynamic-slice_fusion.3
  611.4 3.5 conditional.3
  666.3 3.5 conditional.3
  677.6 2.1 constant_dynamic-slice_fusion.3
  682.0 3.5 conditional.3
  691.5 16.9 %reduce-scatter.2.cloned.1.call-done = bf16[64,2048]{1,0:T(8,128)(2,1)} async-done(((bf16[128,2048]{1,0:T(8,128)(2,1)}), bf16[64,2048]{1,0:T(8,128)(2,1)}) %reduce-scatter.2.cloned.1.call-update) | async-done | bytes 262160 | tf_op jit(solution)/shard_map/reduce_scatter | solution.py:178
  (558 shorter events, 205.8 us)
Async XLA Ops:
  7.2 682.2 %copy-start = (bf16[512,2048]{1,0:T(8,128)(2,1)S(1)}, bf16[512,2048]{1,0:T(8,128)(2,1)}, u32[]{:S(2)}) copy-start(bf16[512,2048]{1,0:T(8,128)(2,1)} %param.18) | copy-start | bytes 6291460
  7.2 4.1 copy-start.5
  7.2 4.1 copy-start.13
  7.2 227.8 %all-gather.5.cloned.1.call-start = ((), (), s32[]{:S(2)}) async-start(), calls=%async_computation.2 | async-start | bytes 8454144 | tf_op jit(solution)/shard_map/all_gather | solution.py:141
  8.6 4.4 copy-start.14
  8.7 10.0 %copy-start.1 = (s32[512]{0:T(512)S(1)}, s32[512]{0:T(512)}, u32[]{:S(2)}) copy-start(s32[512]{0:T(512)} %param.21) | copy-start | bytes 6148
  11.1 446.0 %all-gather.3.cloned.1.call-start = ((), (), s32[]{:S(2)}) async-start(), calls=%async_computation.1 | async-start | bytes 8454144 | tf_op jit(solution)/shard_map/all_gather | solution.py:140
  123.5 584.9 %reduce-scatter.2.cloned.1.call-start = ((), (), s32[]{:S(2)}) async-start(), calls=%async_computation.3 | async-start | bytes 786432 | tf_op jit(solution)/shard_map/reduce_scatter | solution.py:178
  471.4 4.0 copy-start.7
  471.4 4.0 copy-start.9
  497.6 4.0 copy-start.7
  497.6 4.0 copy-start.9
  510.7 4.0 copy-start.9
  526.3 4.0 copy-start.7
  526.3 4.0 copy-start.9
  555.0 4.0 copy-start.7
  555.0 4.0 copy-start.9
  570.7 4.0 copy-start.9
  602.0 4.0 copy-start.9
  617.7 4.0 copy-start.9
  630.8 4.0 copy-start.9
  643.8 4.0 copy-start.9
  656.9 4.0 copy-start.9
  689.4 19.0 %copy-start.6 = (bf16[128,2048]{1,0:T(8,128)(2,1)S(1)}, bf16[128,2048]{1,0:T(8,128)(2,1)}, u32[]{:S(2)}) copy-start(bf16[128,2048]{1,0:T(8,128)(2,1)} %param.13) | copy-start | bytes 1572868
  (115 other events, 208.5 us)
Sparse Core Ops, SparseCore 0:
  11.2 223.7 all-gather.4
  237.5 219.5 all-gather.2
  690.8 17.5 reduce-scatter.1
where the time goes:
time: 720 us; the launch traced here: 717 us
  waiting for transfers between devices  346 us (48%)
  local copies, waits for them, and re-layouts  216 us (30%)
  other arithmetic  60.5 us (8%)
  matrix products  57.7 us (8%)
  loops' own time  22.4 us (3%)
  between operations  14.1 us (2%)
    all_gather x1, waiting for transfers between devices, on_device(): key_piece = lax.all_gather(key_matrix_rows, 'seq', axis=0, tiled=True)  222 us
    all_gather x1, waiting for transfers between devices, on_device(): value_piece = lax.all_gather(value_matrix_rows, 'seq', axis=0, tiled=True)  107 us
    gather x1, local copies, waits for them, and re-layouts, on_device(): slot_ids = page_slot[position // PAGE_TOKENS]  102 us
    dynamic_slice x32, local copies, waits for them, and re-layouts, sub_step(): value_block = lax.dynamic_slice_in_dim(value_piece, offset, sub_width, 0)  49.8 us
    another operation x1, loops' own time, on_device(): lax.scan(sub_step, absorb_state, jnp.arange(length // sub_width, dtype=jn...  22.3 us
    reduce_or x16, other arithmetic, sub_step(): jnp.any(key_target >= 0)  22.2 us
    dynamic_slice x16, local copies, waits for them, and re-layouts, on_device(): lax.scan(sub_step, absorb_state, jnp.arange(length // sub_width, dtype=jn...  21 us
    dynamic_slice x16, local copies, waits for them, and re-layouts, sub_step(): key_block = lax.dynamic_slice_in_dim(key_piece, offset, sub_width, 0)  19.9 us
  transfers between devices with their start and end apart: 3, of which 3 were waited for; matrix products, arithmetic and copies ran while one was open for 16% of the time, Pallas kernels for 0%

commit v1 on v0

--- a/solution.py
+++ b/solution.py
@@ -138,7 +138,9 @@
     state = (start_max, start_sum, start_acc, start_keys, start_values)
     absorb_state = state
     key_piece = lax.all_gather(key_matrix_rows, "seq", axis=0, tiled=True)
-    value_piece = lax.all_gather(value_matrix_rows, "seq", axis=0, tiled=True)
+    value_piece = jnp.concatenate(
+        lax.all_to_all(jnp.stack([value_matrix_rows] * lax.axis_size("seq")), "seq", 0, 0), axis=0
+    )
     length = key_piece.shape[0]
     sub_width = math.gcd(length, 1024)
 

time: 720 us -> 754 us (1.047)
  waiting for transfers between devices: 346 us -> 240 us
  matrix products: 57.7 us -> 123 us
  other arithmetic: 60.5 us -> 97.6 us
  local copies, waits for them, and re-layouts: 216 us -> 235 us
  starting transfers between devices: 0.12 us -> 15.6 us
    all_gather x1 -> x0, waiting for transfers between devices: 107 us -> none  [on_device(): value_piece = lax.all_gather(value_matrix_rows, 'seq', axis=0, tiled=True)]
    all_gather x1, waiting for transfers between devices: 222 us -> 149 us  [on_device(): key_piece = lax.all_gather(key_matrix_rows, 'seq', axis=0, tiled=True)]
    all_to_all x0 -> x1, waiting for transfers between devices: none -> 69.1 us  [on_device(): lax.all_to_all(jnp.stack([value_matrix_rows] * lax.axis_size('seq')), 'se...]
    dot_general x16, matrix products: 14.4 us -> 53.3 us  [attend(): jnp.einsum('hgqk,khd->hgqd', weights.astype(jnp.bfloat16), value_heads, p...]
    dot_general x16, matrix products: 8.18 us -> 43.9 us  [attend(): jnp.einsum('qhgd,khd->hgqk', queries, key_heads, preferred_element_type=j...]
    reduce_sum x16, other arithmetic: 8.53 us -> 33.9 us  [attend(): new_sum = run_sum * factor + jnp.sum(weights, -1)]
    while x272 -> x48, local copies, waits for them, and re-layouts: 18.8 us -> 0.08 us
    all_to_all x0 -> x1, starting transfers between devices: none -> 15.4 us  [on_device(): lax.all_to_all(jnp.stack([value_matrix_rows] * lax.axis_size('seq')), 'se...]
  transfers between devices with their start and end apart: 3 -> 3, of which waited for: 3 -> 3; matrix products, arithmetic and copies ran while one was open for 16% -> 18% of each run, Pallas kernels for 0% -> 0%
where the time goes in v1:
time: 754 us; the launch traced here: 749 us
  waiting for transfers between devices  240 us (32%)
  local copies, waits for them, and re-layouts  235 us (31%)
  matrix products  123 us (16%)
  other arithmetic  97.6 us (13%)
  loops' own time  23.4 us (3%)
  starting transfers between devices  15.6 us (2%)
  between operations  14.4 us (2%)
    all_gather x1, waiting for transfers between devices, on_device(): key_piece = lax.all_gather(key_matrix_rows, 'seq', axis=0, tiled=True)  149 us
    gather x1, local copies, waits for them, and re-layouts, on_device(): slot_ids = page_slot[position // PAGE_TOKENS]  102 us
    all_to_all x1, waiting for transfers between devices, on_device(): lax.all_to_all(jnp.stack([value_matrix_rows] * lax.axis_size('seq')), 'se...  69.1 us
    dot_general x16, matrix products, attend(): jnp.einsum('hgqk,khd->hgqd', weights.astype(jnp.bfloat16), value_heads, p...  53.3 us
    dynamic_slice x32, local copies, waits for them, and re-layouts, sub_step(): value_block = lax.dynamic_slice_in_dim(value_piece, offset, sub_width, 0)  49.2 us
    dot_general x16, matrix products, attend(): jnp.einsum('qhgd,khd->hgqk', queries, key_heads, preferred_element_type=j...  43.9 us
    reduce_sum x16, other arithmetic, attend(): new_sum = run_sum * factor + jnp.sum(weights, -1)  33.9 us
    another operation x1, loops' own time, on_device(): lax.scan(sub_step, absorb_state, jnp.arange(length // sub_width, dtype=jn...  23.1 us
  transfers between devices with their start and end apart: 3, of which 3 were waited for; matrix products, arithmetic and copies ran while one was open for 18% of the time, Pallas kernels for 0%

profile of v1, /device:TPU:1, one launch (start us, length us, event | category | flops | bytes accessed | tf_op | source)
XLA Modules:
  0.0 749.1 jit_solution(1787756860883533870)
XLA Ops:
  10.4 5.3 stack.5
  15.8 15.4 %all-to-all-start = ((bf16[128,128,256]{1,2,0:T(8,128)(2,1)}), bf16[128,128,256]{1,2,0:T(8,128)(2,1)}, u32[]{:S(2)}, u32[]{:S(2)}) async-start(bf16[128,128,256]{1,2,0:T(8,128)(2,1)} %stack.5), calls=%async_computation | async-start | bytes 16777216 | tf_op jit(solution)/shard_map/all_to_all | solution.py:142
  31.3 5.1 select_reduce_fusion
  36.9 101.9 %gather_fusion = s32[16384]{0:T(1024)S(1)} fusion(s32[512]{0:T(512)S(1)} %copy-done.1, s32[16384]{0:T(1024)S(1)} %broadcast_clamp_fusion), kind=kCustom, calls=%fused_computation | custom fusion | bytes 196608 | tf_op jit(solution)/shard_map/gather | solution.py:72
  150.1 69.1 %all-to-all-done = bf16[128,128,256]{1,2,0:T(8,128)(2,1)} async-done(((bf16[128,128,256]{1,2,0:T(8,128)(2,1)}), bf16[128,128,256]{1,2,0:T(8,128)(2,1)}, u32[]{:S(2)}, u32[]{:S(2)}) %all-to-all-start) | async-done | bytes 8388640 | tf_op jit(solution)/shard_map/all_to_all | solution.py:142
  219.2 12.0 %copy.73 = bf16[128,128,256]{2,1,0:T(8,128)(2,1)} copy(bf16[128,128,256]{1,2,0:T(8,128)(2,1)} %all-to-all-done) | data formatting | bytes 16777216 | tf_op jit(solution)/shard_map/all_to_all | solution.py:142
  231.2 149.2 %all-gather.2.cloned.1.call-done = bf16[16384,256]{1,0:T(8,128)(2,1)} async-done(((bf16[128,256]{1,0:T(8,128)(2,1)}), bf16[16384,256]{1,0:T(8,128)(2,1)}) %all-gather.2.cloned.1.call-update) | async-done | bytes 8388624 | tf_op jit(solution)/shard_map/all_gather | solution.py:140
  381.7 334.2 %while.19 = (s32[]{:T(128)}, f32[2,2,128]{2,1,0:T(2,128)S(1)}, f32[2,2,128]{2,1,0:T(2,128)S(1)}, f32[2,2,128,128]{3,2,1,0:T(8,128)}, f32[256,256]{1,0:T(8,128)S(...) while((s32[]{:T(128)}, f32[2,2,128]{2,1,0:T(2,128)S(1)}, ...), condition=%wide.region_11.12_spmd.clone, body=%wide.region_5.11_spmd.clone.sunk | while | flops 544936448 | bytes 16983412 | solution.py:169
  415.5 3.3 convolution_add_fusion.4
  435.2 3.3 convolution_add_fusion.4
  454.9 3.3 convolution_add_fusion.4
  474.6 3.3 convolution_add_fusion.4
  496.7 3.3 convolution_add_fusion.4
  518.7 3.3 convolution_add_fusion.4
  538.4 3.3 convolution_add_fusion.4
  560.5 3.3 convolution_add_fusion.4
  582.6 3.3 convolution_add_fusion.4
  604.7 3.3 convolution_add_fusion.4
  626.8 3.3 convolution_add_fusion.4
  646.5 3.3 convolution_add_fusion.4
  666.2 3.3 convolution_add_fusion.4
  685.9 3.3 convolution_add_fusion.4
  708.0 3.3 convolution_add_fusion.4
  719.1 21.5 %reduce-scatter.2.cloned.1.call-done = bf16[64,2048]{1,0:T(8,128)(2,1)} async-done(((bf16[128,2048]{1,0:T(8,128)(2,1)}), bf16[64,2048]{1,0:T(8,128)(2,1)}) %reduce-scatter.2.cloned.1.call-update) | async-done | bytes 262160 | tf_op jit(solution)/shard_map/reduce_scatter | solution.py:180
  (338 shorter events, 301.5 us)
Async XLA Ops:
  7.2 709.8 %copy-start = (bf16[512,2048]{1,0:T(8,128)(2,1)S(1)}, bf16[512,2048]{1,0:T(8,128)(2,1)}, u32[]{:S(2)}) copy-start(bf16[512,2048]{1,0:T(8,128)(2,1)} %param.18) | copy-start | bytes 6291460
  15.8 15.5 %copy-start.8 = (s32[128]{0:T(128)S(1)}, s32[128]{0:T(128)}, u32[]{:S(2)}) copy-start(s32[128]{0:T(128)} %param.20) | copy-start | bytes 1540
  15.8 203.5 %all-to-all-start = ((bf16[128,128,256]{1,2,0:T(8,128)(2,1)}), bf16[128,128,256]{1,2,0:T(8,128)(2,1)}, u32[]{:S(2)}, u32[]{:S(2)}) async-start(bf16[128,128,256]{1,2,0:T(8,128)(2,1)} %stack.5), calls=%async_computation | async-start | bytes 16777216 | tf_op jit(solution)/shard_map/all_to_all | solution.py:142
  31.1 5.7 copy-start.1
  31.2 349.2 %all-gather.2.cloned.1.call-start = ((), (), s32[]{:S(2)}) async-start(), calls=%async_computation.2 | async-start | bytes 8454144 | tf_op jit(solution)/shard_map/all_gather | solution.py:140
  36.9 102.7 %copy-start.9 = (s32[4]{0:T(128)S(1)}, s32[4]{0:T(128)}, u32[]{:S(2)}) copy-start(s32[4]{0:T(128)} %param.19) | copy-start | bytes 52
  36.9 102.9 %copy-start.4 = (bf16[128,2048]{1,0:T(8,128)(2,1)S(1)}, bf16[128,2048]{1,0:T(8,128)(2,1)}, u32[]{:S(2)}) copy-start(bf16[128,2048]{1,0:T(8,128)(2,1)} %param.13) | copy-start | bytes 1572868
  36.9 102.9 %copy-start.7 = (f32[2048]{0:T(1024)S(1)}, f32[2048]{0:T(1024)}, u32[]{:S(2)}) copy-start(f32[2048]{0:T(1024)} %param.14) | copy-start | bytes 24580
  142.7 88.5 %copy-start.6 = (s32[16384]{0:T(1024)}, s32[16384]{0:T(1024)S(1)}, u32[]{:S(2)}) copy-start(s32[16384]{0:T(1024)S(1)} %convert_reduce_fusion) | copy-start | bytes 196612
  145.7 594.9 %reduce-scatter.2.cloned.1.call-start = ((), (), s32[]{:S(2)}) async-start(), calls=%async_computation.3 | async-start | bytes 786432 | tf_op jit(solution)/shard_map/reduce_scatter | solution.py:180
  415.5 5.4 copy-start.2
  435.2 5.4 copy-start.2
  454.9 5.4 copy-start.2
  496.7 5.4 copy-start.2
  518.7 5.4 copy-start.2
  538.4 5.4 copy-start.2
  560.5 5.4 copy-start.2
  582.6 5.4 copy-start.2
  604.7 5.4 copy-start.2
  626.8 5.4 copy-start.2
  646.5 5.4 copy-start.2
  666.2 5.4 copy-start.2
  685.9 5.4 copy-start.2
  717.0 23.6 %copy-start.5 = (bf16[128,2048]{1,0:T(8,128)(2,1)S(1)}, bf16[128,2048]{1,0:T(8,128)(2,1)}, u32[]{:S(2)}) copy-start(bf16[128,2048]{1,0:T(8,128)(2,1)} %param.13) | copy-start | bytes 1572868
  (4 other events, 17.6 us)
Sparse Core Ops, SparseCore 0:
  145.8 234.4 all-gather.1
  718.4 22.1 reduce-scatter.1
